TPU v7x, 32 devices: a whole 2x2x4 slice. The times are simulated.
32 devices in a mesh: loop: 8 (over z, core), red: 4 (over y, x).
Axes of the slice: x: 2, y: 2, z: 4, core: 2. Of those that a mesh axis runs over, the one named last changes fastest.
Arguments:
- query_ids: int32 [512], replicated, may hold values from 0 to 8191
- layer_index: int32 [1], replicated, may hold values from 0 to 3
- gradient: bfloat16 [8192, 28672], P('loop', 'red'), may hold values from -6 to 6
- out_basis: bfloat16 [8192, 8192], P('loop'), may hold values from -0.0625 to 0.0625
- in_basis: bfloat16 [28672, 28672], P('red', 'loop'), may hold values from -0.03125 to 0.03125
- out_eigen: float32 [4, 8192], replicated, may hold values from 0.2 to 2
- in_eigen: float32 [4, 28672], P(None, 'loop'), may hold values from 0.2 to 2
Outputs:
- preconditioned: bfloat16 [512, 28672], P('loop', 'red')
All inputs are finite; a program needn't handle non-finite values.
Results may differ from a plain program's by a relative error of at most 0.0055.
Values may be sent and summed in bfloat16 or wider, within the bound.
A program may use at most 192 MiB of HBM per device.

v0:
```python
import jax
import jax.numpy as jnp
from jax import lax
from jax.experimental import pallas as pl
from jax.experimental.pallas import tpu as pltpu
from jax.sharding import PartitionSpec as P

damping = 0.05
QUERY_CHUNKS = 2
PIECES = 14
IN_LAG, MID_LAG, OUT_LAG, SCATTER_LAG = 1, 2, 2, 1


def piece_count(*sizes):
    count = PIECES
    while any(size % count or (size // count) % 128 for size in sizes):
        count -= 1
    return count


def make(mesh):
    loop, red = mesh.shape["loop"], mesh.shape["red"]
    chips = loop // 2
    half = chips // 2
    bits = red.bit_length() - 1
    f32, bf16 = jnp.float32, jnp.bfloat16

    def product(per, own, r, depth, rows, cols, n):
        wide, thin = rows // n, cols // n
        total = QUERY_CHUNKS * n
        sum_lag = 2 + (IN_LAG + OUT_LAG) * (half - 1) + MID_LAG
        sum_slots = sum_lag + 1
        red_lag = 2 * bits
        red_slots = red_lag + 2
        scatter_lag = 1 + (chips - 1) * SCATTER_LAG
        scatter_slots = scatter_lag + 3
        stream = per // 2
        turn_at, out_at = [], []
        for q in range(QUERY_CHUNKS):
            ready = (q + 1) * n + sum_lag
            turn_at.append(max(ready, turn_at[-1] + n) if q else ready)
            ready = turn_at[-1] + n + red_lag
            out_at.append(max(ready, out_at[-1] + n) if q else ready)
        ticks = out_at[-1] + n + scatter_lag

        def kernel(
            selected, gradient, in_basis, eigen_rows, eigen_cols, out,
            grad_tile, mine, other, swapped, arrived, crossed, sent, rows_w,
            turn_tile, part, staged, *rest,
        ):
            got, rest = rest[:bits], rest[bits:]
            (
                scaled, out_tile, omine, oother, oswapped, rsent, lsent, rgot, lgot,
                grad_sem, turn_sem, tile_sem,
                swap_s, swap_r, in_s, in_r, mid_s, mid_r, out_s, out_r, back_s, back_r,
                red_s, red_r, all_s, all_r,
                oswap_s, oswap_r, right_s, right_r, left_s, left_r,
            ) = rest
            me = lax.axis_index("loop")
            here = lax.axis_index("red")
            chip, core = me // 2, me % 2
            left = chip < half
            depth_in = jnp.where(left, chip, chips - 1 - chip)
            is_mid = depth_in == half - 1
            is_end = depth_in == 0
            partner = chip * 2 + 1 - core
            inner = jnp.where(left, me + 2, me - 2)
            outer = jnp.where(left, me - 2, me + 2)

            def remote(src, dst, s, r, k, to):
                return pltpu.make_async_remote_copy(
                    src_ref=src, dst_ref=dst, send_sem=s.at[k], recv_sem=r.at[k],
                    device_id=to, device_id_type=pl.DeviceIdType.MESH,
                )

            def span(i, size):
                return pl.ds(pl.multiple_of(i * size, size), size)

            def swap(g):
                s = g % sum_slots
                return remote(other.at[s], swapped.at[s], swap_s, swap_r, s, {"loop": partner})

            def go_in(g):
                s = g % sum_slots
                return remote(sent.at[s], arrived.at[s], in_s, in_r, s, {"loop": inner})

            def go_mid(g):
                s = g % sum_slots
                return remote(sent.at[s], crossed.at[s], mid_s, mid_r, s, {"loop": inner})

            def go_out(g):
                at = rows_w.at[g // n, pl.ds(0, own), span(g % n, wide)]
                return remote(at, at, out_s, out_r, g % sum_slots, {"loop": outer})

            def go_back(g):
                cut = span(g % n, wide)
                return remote(
                    rows_w.at[g // n, pl.ds(0, own), cut], rows_w.at[g // n, pl.ds(own, own), cut],
                    back_s, back_r, g % sum_slots, {"loop": partner},
                )

            order = [[(k + turn) % bits for k in range(bits)] for turn in range(2)]
            keep, give = [], []
            for turn in range(2):
                at = turn * stream
                keep.append([at])
                give.append([])
                for k, bit in enumerate(order[turn]):
                    size = stream >> (k + 1)
                    mine_is = (here // (1 << bit)) % 2
                    give[turn].append(at + (1 - mine_is) * size)
                    at = at + mine_is * size
                    keep[turn].append(at)

            def across(turn, k):
                bit = 1 << order[turn][k]
                up = (here // bit) % 2
                return {"red": here + bit - 2 * bit * up}

            def held(start, k):
                size = stream >> k
                return pl.ds(pl.multiple_of(start, size), size)

            def red_send(g, turn, k):
                s = g % red_slots
                return remote(
                    staged.at[s, held(give[turn][k], k + 1)], got[k].at[s, turn],
                    red_s, red_r, (k * 2 + turn) * red_slots + s, across(turn, k),
                )

            def all_send(g, turn, k):
                at = scaled.at[g // n, held(keep[turn][k + 1], k + 1), span(g % n, thin)]
                return remote(
                    at, at, all_s, all_r, (k * 2 + turn) * red_slots + g % red_slots, across(turn, k)
                )

            def out_swap(g):
                s = g % scatter_slots
                return remote(oother.at[s], oswapped.at[s], oswap_s, oswap_r, s, {"loop": partner})

            def go_right(g, b):
                s = g % scatter_slots
                return remote(
                    rsent.at[s, span(b, r)], rgot.at[s, span(b, r)], right_s, right_r,
                    s * chips + b, {"loop": me + 2},
                )

            def go_left(g, b):
                s = g % scatter_slots
                return remote(
                    lsent.at[s, span(b, r)], lgot.at[s, span(b, r)], left_s, left_r,
                    s * chips + b, {"loop": me - 2},
                )

            barrier = pltpu.get_barrier_semaphore()

            def greet(to):
                pl.semaphore_signal(
                    barrier, inc=1, device_id=to, device_id_type=pl.DeviceIdType.MESH
                )

            greet({"loop": partner})
            for k in range(bits):
                greet(across(0, k))
            pl.when(chip > 0)(lambda: greet({"loop": me - 2}))
            pl.when(chip < chips - 1)(lambda: greet({"loop": me + 2}))
            edge = (chip == 0) | (chip == chips - 1)
            pl.semaphore_wait(barrier, 1 + bits + jnp.where(edge, 1, 2))

            def fetch_grad(g):
                return pltpu.make_async_copy(
                    gradient.at[:, span(g % n, wide)], grad_tile.at[g % 2], grad_sem.at[g % 2]
                )

            def fetch_turn(g):
                return pltpu.make_async_copy(
                    in_basis.at[:, span(g % n, thin)], turn_tile.at[g % 2], turn_sem.at[g % 2]
                )

            def fetch_out(g):
                return pltpu.make_async_copy(
                    in_basis.at[span(g % n, wide)], out_tile.at[g % 2], tile_sem.at[g % 2]
                )

            def ahead(fetch, g):
                fetch(g).wait()
                pl.when(g + 1 < total)(lambda: fetch(g + 1).start())

            def rows_tile(g):
                s = g % sum_slots
                ahead(fetch_grad, g)
                whole = jnp.dot(
                    selected[g // n], grad_tile[g % 2], preferred_element_type=f32
                )
                pl.when(g >= sum_slots)(lambda: swap(g - sum_slots).wait_send())
                mine[s] = whole[:own]
                other[s] = whole[own:].astype(bf16)
                swap(g).start()

            def sum_in(g):
                s = g % sum_slots

                @pl.when(g >= sum_slots)
                def _():
                    pl.when(is_mid)(lambda: go_mid(g - sum_slots).wait_send())
                    pl.when(jnp.logical_not(is_mid))(lambda: go_in(g - sum_slots).wait_send())

                swap(g).wait_recv()

                @pl.when(is_end)
                def _():
                    value = mine[s] + swapped[s].astype(f32)
                    mine[s] = value
                    sent[s] = value.astype(bf16)

                @pl.when(jnp.logical_not(is_end))
                def _():
                    go_in(g).wait_recv()
                    value = mine[s] + swapped[s].astype(f32) + arrived[s].astype(f32)
                    mine[s] = value
                    sent[s] = value.astype(bf16)

                pl.when(is_mid)(lambda: go_mid(g).start())
                pl.when(jnp.logical_not(is_mid))(lambda: go_in(g).start())

            def sum_out(g):
                s = g % sum_slots

                @pl.when(g >= sum_slots)
                def _():
                    go_back(g - sum_slots).wait_send()
                    pl.when(jnp.logical_not(is_end))(lambda: go_out(g - sum_slots).wait_send())

                @pl.when(is_mid)
                def _():
                    go_mid(g).wait_recv()
                    value = (mine[s] + crossed[s].astype(f32)).astype(bf16)
                    rows_w[g // n, pl.ds(0, own), span(g % n, wide)] = value

                pl.when(jnp.logical_not(is_mid))(lambda: go_out(g).wait_recv())
                pl.when(jnp.logical_not(is_end))(lambda: go_out(g).start())
                go_back(g).start()

            def hand_over(g, k):
                s = g % red_slots
                for turn in range(2):
                    pl.when(g >= red_slots)(
                        lambda turn=turn: red_send(g - red_slots, turn, k).wait_send()
                    )
                    at = held(give[turn][k], k + 1)
                    staged[s, at] = part[s, at].astype(bf16)
                    red_send(g, turn, k).start()

            def turn_tile_of(g):
                s = g % red_slots
                ahead(fetch_turn, g)
                cut = rows // 4

                def some(j):
                    at = span(j, cut)
                    return jnp.dot(
                        rows_w[g // n, :, at], turn_tile[g % 2, at], preferred_element_type=f32
                    )

                part[s] = some(0)

                def more(j, c):
                    part[s] += some(j)
                    return c

                lax.fori_loop(1, 4, more, 0)
                hand_over(g, 0)

            def red_in(g, k):
                s = g % red_slots
                cut = span(g % n, thin)
                for turn in range(2):
                    red_send(g, turn, k).wait_recv()
                    at = held(keep[turn][k + 1], k + 1)
                    value = part[s, at] + got[k][s, turn].astype(f32)
                    if k + 1 < bits:
                        part[s, at] = value
                    else:
                        pl.when(g >= red_slots)(
                            lambda turn=turn: all_send(g - red_slots, turn, k).wait_send()
                        )
                        scale = eigen_rows[g // n, at] * eigen_cols[:, cut]
                        scaled[g // n, at, cut] = (value / (scale + damping)).astype(bf16)
                        all_send(g, turn, k).start()
                if k + 1 < bits:
                    hand_over(g, k + 1)

            def red_out(g, k):
                for turn in range(2):
                    all_send(g, turn, k).wait_recv()
                    if k > 0:
                        pl.when(g >= red_slots)(
                            lambda turn=turn: all_send(g - red_slots, turn, k - 1).wait_send()
                        )
                        all_send(g, turn, k - 1).start()

            def out_tile_of(g):
                s = g % scatter_slots
                ahead(fetch_out, g)
                pl.when(g >= scatter_slots)(lambda: out_swap(g - scatter_slots).wait_send())
                whole = lax.dot_general(
                    scaled[g // n], out_tile[g % 2], (((1,), (1,)), ((), ())),
                    preferred_element_type=f32,
                )
                omine[s] = whole[:own]
                oother[s] = whole[own:].astype(bf16)
                out_swap(g).start()

            def each(start, stop, f):
                lax.fori_loop(start, stop, lambda b, c: (f(b), c)[1], 0)

            def chip_sum(g):
                s = g % scatter_slots
                out_swap(g).wait_recv()
                omine[s] += oswapped[s].astype(f32)

            def flow(g, go, send, get, first, start, stop):
                s = g % scatter_slots

                @pl.when(first)
                def _():
                    def plain(b):
                        pl.when(g >= scatter_slots)(lambda: go(g - scatter_slots, b).wait_send())
                        send[s, span(b, r)] = omine[s, span(b, r)].astype(bf16)
                        go(g, b).start()

                    each(start, stop, plain)

                @pl.when(jnp.logical_not(first))
                def _():
                    go(g, chip).wait_recv()
                    mid = span(chip, r)

                    def through(b):
                        pl.when(g >= scatter_slots)(lambda: go(g - scatter_slots, b).wait_send())
                        go(g, b).wait_recv()
                        at = span(b, r)
                        send[s, at] = (omine[s, at] + get[s, at].astype(f32)).astype(bf16)
                        go(g, b).start()

                    each(start, stop, through)
                    omine[s, mid] += get[s, mid].astype(f32)

            def finish(g):
                s = g % scatter_slots
                out[span(g // n, r), span(g % n, wide)] = omine[s, span(chip, r)].astype(bf16)

            def when(t, starts, lag, f):
                u = t - lag
                late = u >= starts[1]
                i = u - jnp.where(late, starts[1], starts[0])
                g = i + jnp.where(late, n, 0)
                pl.when((i >= 0) & (i < n))(lambda: f(g))

            fetch_grad(0).start()
            fetch_turn(0).start()
            fetch_out(0).start()
            row_at = [0, n]

            def tick(t):
                when(t, row_at, 0, rows_tile)
                when(t, turn_at, 0, turn_tile_of)
                when(t, out_at, 0, out_tile_of)
                when(t, row_at, 1 + IN_LAG * depth_in, sum_in)
                mid_at = 1 + IN_LAG * (half - 1) + MID_LAG
                when(t, row_at, mid_at + OUT_LAG * (half - 1 - depth_in), sum_out)
                when(t, row_at, sum_lag, lambda g: go_back(g).wait_recv())
                when(t, out_at, 1, chip_sum)
                when(
                    t, out_at, 1 + SCATTER_LAG * chip,
                    lambda g: flow(g, go_right, rsent, rgot, chip == 0, chip + 1, chips),
                )
                when(
                    t, out_at, 1 + SCATTER_LAG * (chips - 1 - chip),
                    lambda g: flow(g, go_left, lsent, lgot, chip == chips - 1, 0, chip),
                )
                for k in range(bits):
                    when(t, turn_at, 1 + k, lambda g, k=k: red_in(g, k))
                for k in range(bits):
                    when(t, turn_at, 1 + bits + k, lambda g, k=k: red_out(g, bits - 1 - k))
                last = 1 + SCATTER_LAG * jnp.maximum(chip, chips - 1 - chip)
                when(t, out_at, last, finish)

            each(0, ticks, tick)

            def drain_sum(g):
                swap(g).wait_send()
                go_back(g).wait_send()
                pl.when(is_mid)(lambda: go_mid(g).wait_send())
                pl.when(jnp.logical_not(is_mid))(lambda: go_in(g).wait_send())
                pl.when(jnp.logical_not(is_end))(lambda: go_out(g).wait_send())

            def drain_red(g):
                for turn in range(2):
                    for k in range(bits):
                        red_send(g, turn, k).wait_send()
                        all_send(g, turn, k).wait_send()

            def drain_scatter(g):
                out_swap(g).wait_send()
                each(chip + 1, chips, lambda b: go_right(g, b).wait_send())
                each(0, chip, lambda b: go_left(g, b).wait_send())

            each(max(0, total - sum_slots), total, drain_sum)
            each(max(0, total - red_slots), total, drain_red)
            each(max(0, total - scatter_slots), total, drain_scatter)

        vmem = pl.BlockSpec(memory_space=pltpu.VMEM)
        hbm = pl.BlockSpec(memory_space=pl.ANY)

        def sems(count):
            return pltpu.SemaphoreType.DMA((count,))

        def slots(count, *shape):
            return pltpu.VMEM((count, *shape), bf16)

        return pl.pallas_call(
            kernel,
            out_shape=jax.ShapeDtypeStruct((QUERY_CHUNKS * r, rows), bf16),
            in_specs=[vmem, hbm, hbm, vmem, vmem],
            out_specs=vmem,
            scratch_shapes=[slots(2, depth, wide), pltpu.VMEM((sum_slots, own, wide), f32)]
            + [slots(sum_slots, own, wide)] * 5
            + [
                slots(QUERY_CHUNKS, per, rows),
                slots(2, rows, thin),
                pltpu.VMEM((red_slots, per, thin), f32),
                slots(red_slots, per, thin),
            ]
            + [slots(red_slots, 2, stream >> (k + 1), thin) for k in range(bits)]
            + [
                slots(QUERY_CHUNKS, per, cols),
                slots(2, wide, cols),
                pltpu.VMEM((scatter_slots, own, wide), f32),
            ]
            + [slots(scatter_slots, own, wide)] * 6
            + [sems(2)] * 3
            + [sems(sum_slots)] * 10
            + [sems(2 * bits * red_slots)] * 4
            + [sems(scatter_slots)] * 2
            + [sems(scatter_slots * chips)] * 4,
            compiler_params=pltpu.CompilerParams(
                collective_id=0, has_side_effects=True, vmem_limit_bytes=62 * 1024 * 1024
            ),
        )

    def per_device(query_ids, layer_index, gradient, out_basis, in_basis, out_eigen, in_eigen):
        core = lax.axis_index("loop") % 2
        queries = query_ids.shape[0]
        depth, rows = gradient.shape
        cols = in_basis.shape[1]
        r = queries // loop // QUERY_CHUNKS
        per = queries // QUERY_CHUNKS
        ids = query_ids.reshape(chips, 2, QUERY_CHUNKS, r).transpose(2, 1, 0, 3)
        ids = jnp.where(core == 0, ids, ids[:, ::-1]).reshape(-1)
        out_row = lax.dynamic_index_in_dim(out_eigen, layer_index[0], 0, keepdims=False)
        eigen_cols = lax.dynamic_index_in_dim(in_eigen, layer_index[0], 0)
        eigen_rows = jnp.take(out_row, ids).reshape(QUERY_CHUNKS, per, 1)
        every = lax.broadcasted_iota(jnp.int32, (queries, out_basis.shape[1]), 1)
        selected = lax.dot_general(
            (ids[:, None] == every).astype(bf16), out_basis,
            (((1,), (1,)), ((), ())), preferred_element_type=f32,
        ).astype(bf16)
        selected = selected.reshape(QUERY_CHUNKS, per, depth)
        run = product(per, per // 2, r, depth, rows, cols, piece_count(rows, cols))
        return run(selected, gradient, in_basis, eigen_rows, eigen_cols)

    return per_device


def solution(mesh):
    return jax.shard_map(
        make(mesh),
        mesh=mesh,
        in_specs=(
            P(),
            P(),
            P("loop", "red"),
            P("loop", None),
            P("red", "loop"),
            P(),
            P(None, "loop"),
        ),
        out_specs=P("loop", "red"),
        check_vma=False,
    )
```

profile of v0, /device:TPU:0, one launch (start us, length us, event | category | flops | bytes accessed | tf_op | source)
XLA Modules:
  0.0 252.8 jit_solution(11723728930757957744)
XLA Ops:
  0.0 0.0 copy-start
  0.7 0.8 reshape.94
  1.5 0.1 reshape.97
  1.6 0.1 eq.16
  1.7 1.4 constant_dynamic-slice_fusion.eigen_cols
  3.1 0.0 copy-done
  3.1 3.1 %gather_fusion = f32[512]{0:T(512)S(1)} fusion(f32[8192]{0:T(1024)S(1)} %bitcast.9, s32[1024]{0:T(1024)S(1)} %pad_clamp_fusion), kind=kCustom, calls=%fused_computation | custom fusion | bytes 6144 | tf_op jit(solution)/shard_map/jit(_take)/gather | solution.py:463
  6.3 0.3 reshape.106
  6.6 0.2 gather.10
  6.8 0.8 and_select_fusion.eigen_rows
  7.5 12.9 %fusion.2 = bf16[512,1024]{1,0:T(8,128)(2,1)} fusion(bf16[1024,8192]{1,0:T(8,128)(2,1)} %param.10, s32[512]{0:T(512)S(1)} %eq.16), kind=kOutput, calls=%fused_computation.4 | convolution fusion | flops 8594653184 | bytes 17827840 | tf_op jit(solution)/shard_map/dot_general | solution.py:465
  20.4 0.0 copy-start.1
  20.4 230.2 %shard_map.73 = bf16[64,7168]{1,0:T(8,128)(2,1)} custom-call(bf16[2,256,1024]{2,1,0:T(8,128)(2,1)} %bitcast.10, bf16[1024,7168]{1,0:T(8,128)(2,1)} %gradient.1, bf16[7168,3584]{1,0:T(8,128)(2,1)} %in_basis.1, f32[2,256,1]{2,1,0:T(8,128)} %and_select_fusion.eigen_rows, f32[1,3584]{1,0:T(1,128)} %constant_dynamic-slice_fusion.eigen_cols), custom_call_target="tpu_custom_call" | custom-call | tf_op jit(solution)/shard_map/pallas_call | solution.py:471
  250.6 2.2 copy.22
  252.8 0.0 copy-done.1
  (5 shorter events, 0.1 us)
Async XLA Ops:
  0.0 3.1 %copy-start = (f32[4,8192]{1,0:T(4,128)S(1)}, f32[4,8192]{1,0:T(4,128)}, u32[]{:S(2)}) copy-start(f32[4,8192]{1,0:T(4,128)} %param.12) | copy-start | bytes 393220
  20.4 232.4 %copy-start.1 = (f32[4,8192]{1,0:T(4,128)S(1)}, f32[4,8192]{1,0:T(4,128)}, u32[]{:S(2)}) copy-start(f32[4,8192]{1,0:T(4,128)} %param.12) | copy-start | bytes 393220
where the time goes:
time: 253 us
  Pallas kernels  230 us (91%)
  matrix products  12.9 us (5%)
  local copies, waits for them, and re-layouts  8.17 us (3%)
    pallas_call x1, Pallas kernels, per_device(): return run(selected, gradient, in_basis, eigen_rows, eigen_cols)  230 us
    dot_general x1, matrix products, per_device(): lax.dot_general((ids[:, None] == every).astype(bf16), out_basis, (((1,),...  12.9 us

commit v1 on v0

--- a/solution.py
+++ b/solution.py
@@ -8,7 +8,11 @@
 damping = 0.05
 QUERY_CHUNKS = 2
 PIECES = 14
-IN_LAG, MID_LAG, OUT_LAG, SCATTER_LAG = 1, 2, 2, 1
+IN_LAG, MID_LAG, OUT_LAG, SCATTER_LAG = 2, 2, 2, 2
+BUFFERS = 3
+DEPTHS = 2
+TURN_RATE = (1, 1)
+RED_LAG = 2
 
 
 def piece_count(*sizes):
@@ -30,16 +34,17 @@
         total = QUERY_CHUNKS * n
         sum_lag = 2 + (IN_LAG + OUT_LAG) * (half - 1) + MID_LAG
         sum_slots = sum_lag + 1
-        red_lag = 2 * bits
-        red_slots = red_lag + 2
+        red_lag = 2 * bits * RED_LAG
+        red_slots = -(-(red_lag + 2) * TURN_RATE[0] // TURN_RATE[1])
         scatter_lag = 1 + (chips - 1) * SCATTER_LAG
         scatter_slots = scatter_lag + 3
         stream = per // 2
         turn_at, out_at = [], []
         for q in range(QUERY_CHUNKS):
             ready = (q + 1) * n + sum_lag
-            turn_at.append(max(ready, turn_at[-1] + n) if q else ready)
-            ready = turn_at[-1] + n + red_lag
+            turn_at.append(ready)
+            num, den = (1, 1) if q else TURN_RATE
+            ready = turn_at[-1] + -(-n * den // num) + red_lag
             out_at.append(max(ready, out_at[-1] + n) if q else ready)
         ticks = out_at[-1] + n + scatter_lag
 
@@ -169,28 +174,29 @@
 
             def fetch_grad(g):
                 return pltpu.make_async_copy(
-                    gradient.at[:, span(g % n, wide)], grad_tile.at[g % 2], grad_sem.at[g % 2]
+                    gradient.at[:, span(g % n, wide)], grad_tile.at[g % BUFFERS], grad_sem.at[g % BUFFERS]
                 )
 
             def fetch_turn(g):
                 return pltpu.make_async_copy(
-                    in_basis.at[:, span(g % n, thin)], turn_tile.at[g % 2], turn_sem.at[g % 2]
+                    in_basis.at[:, span(g % n, thin)], turn_tile.at[g % BUFFERS], turn_sem.at[g % BUFFERS]
                 )
 
             def fetch_out(g):
                 return pltpu.make_async_copy(
-                    in_basis.at[span(g % n, wide)], out_tile.at[g % 2], tile_sem.at[g % 2]
+                    in_basis.at[span(g % n, wide)], out_tile.at[g % BUFFERS], tile_sem.at[g % BUFFERS]
                 )
 
             def ahead(fetch, g):
                 fetch(g).wait()
-                pl.when(g + 1 < total)(lambda: fetch(g + 1).start())
+                more = g + BUFFERS - 1
+                pl.when(more < total)(lambda: fetch(more).start())
 
             def rows_tile(g):
                 s = g % sum_slots
                 ahead(fetch_grad, g)
                 whole = jnp.dot(
-                    selected[g // n], grad_tile[g % 2], preferred_element_type=f32
+                    selected[g // n], grad_tile[g % BUFFERS], preferred_element_type=f32
                 )
                 pl.when(g >= sum_slots)(lambda: swap(g - sum_slots).wait_send())
                 mine[s] = whole[:own]
@@ -254,12 +260,12 @@
             def turn_tile_of(g):
                 s = g % red_slots
                 ahead(fetch_turn, g)
-                cut = rows // 4
+                cut = rows // DEPTHS
 
                 def some(j):
                     at = span(j, cut)
                     return jnp.dot(
-                        rows_w[g // n, :, at], turn_tile[g % 2, at], preferred_element_type=f32
+                        rows_w[g // n, :, at], turn_tile[g % BUFFERS, at], preferred_element_type=f32
                     )
 
                 part[s] = some(0)
@@ -268,7 +274,7 @@
                     part[s] += some(j)
                     return c
 
-                lax.fori_loop(1, 4, more, 0)
+                lax.fori_loop(1, DEPTHS, more, 0)
                 hand_over(g, 0)
 
             def red_in(g, k):
@@ -304,7 +310,7 @@
                 ahead(fetch_out, g)
                 pl.when(g >= scatter_slots)(lambda: out_swap(g - scatter_slots).wait_send())
                 whole = lax.dot_general(
-                    scaled[g // n], out_tile[g % 2], (((1,), (1,)), ((), ())),
+                    scaled[g // n], out_tile[g % BUFFERS], (((1,), (1,)), ((), ())),
                     preferred_element_type=f32,
                 )
                 omine[s] = whole[:own]
@@ -352,15 +358,20 @@
 
             def when(t, starts, lag, f):
                 u = t - lag
-                late = u >= starts[1]
-                i = u - jnp.where(late, starts[1], starts[0])
-                g = i + jnp.where(late, n, 0)
-                pl.when((i >= 0) & (i < n))(lambda: f(g))
-
-            fetch_grad(0).start()
-            fetch_turn(0).start()
-            fetch_out(0).start()
-            row_at = [0, n]
+                for q in range(QUERY_CHUNKS):
+                    num, den = TURN_RATE if starts is turn_at and q == 0 else (1, 1)
+
+                    def first(u):
+                        return jnp.clip(u - starts[q], 0, n) * num // den
+
+                    lo, hi = jnp.minimum(first(u), n), jnp.minimum(first(u + 1), n)
+                    each(lo + q * n, hi + q * n, f)
+
+            for g in range(BUFFERS - 1):
+                for fetch in (fetch_grad, fetch_turn, fetch_out):
+                    fetch(g).start()
+
+            row_at = [q * n for q in range(QUERY_CHUNKS)]
 
             def tick(t):
                 when(t, row_at, 0, rows_tile)
@@ -380,9 +391,12 @@
                     lambda g: flow(g, go_left, lsent, lgot, chip == chips - 1, 0, chip),
                 )
                 for k in range(bits):
-                    when(t, turn_at, 1 + k, lambda g, k=k: red_in(g, k))
+                    when(t, turn_at, RED_LAG * (1 + k), lambda g, k=k: red_in(g, k))
                 for k in range(bits):
-                    when(t, turn_at, 1 + bits + k, lambda g, k=k: red_out(g, bits - 1 - k))
+                    when(
+                        t, turn_at, RED_LAG * (1 + bits + k),
+                        lambda g, k=k: red_out(g, bits - 1 - k),
+                    )
                 last = 1 + SCATTER_LAG * jnp.maximum(chip, chips - 1 - chip)
                 when(t, out_at, last, finish)
 
@@ -424,22 +438,22 @@
             out_shape=jax.ShapeDtypeStruct((QUERY_CHUNKS * r, rows), bf16),
             in_specs=[vmem, hbm, hbm, vmem, vmem],
             out_specs=vmem,
-            scratch_shapes=[slots(2, depth, wide), pltpu.VMEM((sum_slots, own, wide), f32)]
+            scratch_shapes=[slots(BUFFERS, depth, wide), pltpu.VMEM((sum_slots, own, wide), f32)]
             + [slots(sum_slots, own, wide)] * 5
             + [
                 slots(QUERY_CHUNKS, per, rows),
-                slots(2, rows, thin),
+                slots(BUFFERS, rows, thin),
                 pltpu.VMEM((red_slots, per, thin), f32),
                 slots(red_slots, per, thin),
             ]
             + [slots(red_slots, 2, stream >> (k + 1), thin) for k in range(bits)]
             + [
                 slots(QUERY_CHUNKS, per, cols),
-                slots(2, wide, cols),
+                slots(BUFFERS, wide, cols),
                 pltpu.VMEM((scatter_slots, own, wide), f32),
             ]
             + [slots(scatter_slots, own, wide)] * 6
-            + [sems(2)] * 3
+            + [sems(BUFFERS)] * 3
             + [sems(sum_slots)] * 10
             + [sems(2 * bits * red_slots)] * 4
             + [sems(scatter_slots)] * 2

time: 253 us -> 225 us (0.89)
  Pallas kernels: 230 us -> 202 us
    pallas_call x1, Pallas kernels: 230 us -> 202 us  [per_device(): return run(selected, gradient, in_basis, eigen_rows, eigen_cols)]
where the time goes in v1:
time: 225 us
  Pallas kernels  202 us (90%)
  matrix products  12.9 us (6%)
  local copies, waits for them, and re-layouts  8.17 us (4%)
    pallas_call x1, Pallas kernels, per_device(): return run(selected, gradient, in_basis, eigen_rows, eigen_cols)  202 us
    dot_general x1, matrix products, per_device(): lax.dot_general((ids[:, None] == every).astype(bf16), out_basis, (((1,),...  12.9 us

profile of v1, /device:TPU:0, one launch (start us, length us, event | category | flops | bytes accessed | tf_op | source)
XLA Modules:
  0.0 224.6 jit_solution(8020209860741044368)
XLA Ops:
  0.0 0.0 copy-start
  0.7 0.8 reshape.94
  1.5 0.1 reshape.97
  1.6 0.1 eq.16
  1.7 1.4 constant_dynamic-slice_fusion.eigen_cols
  3.1 0.0 copy-done
  3.1 3.1 %gather_fusion = f32[512]{0:T(512)S(1)} fusion(f32[8192]{0:T(1024)S(1)} %bitcast.9, s32[1024]{0:T(1024)S(1)} %pad_clamp_fusion), kind=kCustom, calls=%fused_computation | custom fusion | bytes 6144 | tf_op jit(solution)/shard_map/jit(_take)/gather | solution.py:477
  6.3 0.3 reshape.106
  6.6 0.2 gather.10
  6.8 0.8 and_select_fusion.eigen_rows
  7.5 12.9 %fusion.2 = bf16[512,1024]{1,0:T(8,128)(2,1)} fusion(bf16[1024,8192]{1,0:T(8,128)(2,1)} %param.10, s32[512]{0:T(512)S(1)} %eq.16), kind=kOutput, calls=%fused_computation.4 | convolution fusion | flops 8594653184 | bytes 17827840 | tf_op jit(solution)/shard_map/dot_general | solution.py:479
  20.4 0.0 copy-start.1
  20.4 202.0 %shard_map.73 = bf16[64,7168]{1,0:T(8,128)(2,1)} custom-call(bf16[2,256,1024]{2,1,0:T(8,128)(2,1)} %bitcast.10, bf16[1024,7168]{1,0:T(8,128)(2,1)} %gradient.1, bf16[7168,3584]{1,0:T(8,128)(2,1)} %in_basis.1, f32[2,256,1]{2,1,0:T(8,128)} %and_select_fusion.eigen_rows, f32[1,3584]{1,0:T(1,128)} %constant_dynamic-slice_fusion.eigen_cols), custom_call_target="tpu_custom_call" | custom-call | tf_op jit(solution)/shard_map/pallas_call | solution.py:485
  222.4 2.2 copy.22
  224.6 0.0 copy-done.1
  (5 shorter events, 0.1 us)
Async XLA Ops:
  0.0 3.1 %copy-start = (f32[4,8192]{1,0:T(4,128)S(1)}, f32[4,8192]{1,0:T(4,128)}, u32[]{:S(2)}) copy-start(f32[4,8192]{1,0:T(4,128)} %param.12) | copy-start | bytes 393220
  20.4 204.2 %copy-start.1 = (f32[4,8192]{1,0:T(4,128)S(1)}, f32[4,8192]{1,0:T(4,128)}, u32[]{:S(2)}) copy-start(f32[4,8192]{1,0:T(4,128)} %param.12) | copy-start | bytes 393220

commit v2 on v1

--- a/solution.py
+++ b/solution.py
@@ -10,6 +10,7 @@
 PIECES = 14
 IN_LAG, MID_LAG, OUT_LAG, SCATTER_LAG = 2, 2, 2, 2
 BUFFERS = 3
+PICK_BUFFERS, TURN_BUFFERS, OUT_BUFFERS = 6, 3, 2
 DEPTHS = 2
 TURN_RATE = (1, 1)
 RED_LAG = 2
@@ -29,15 +30,16 @@
     bits = red.bit_length() - 1
     f32, bf16 = jnp.float32, jnp.bfloat16
 
-    def product(per, own, r, depth, rows, cols, n):
+    def product(per, own, r, depth, units, rows, cols, n):
         wide, thin = rows // n, cols // n
         total = QUERY_CHUNKS * n
+        picks = units // wide
         sum_lag = 2 + (IN_LAG + OUT_LAG) * (half - 1) + MID_LAG
         sum_slots = sum_lag + 1
         red_lag = 2 * bits * RED_LAG
-        red_slots = -(-(red_lag + 2) * TURN_RATE[0] // TURN_RATE[1])
+        red_slots = -(-(red_lag + 1) * TURN_RATE[0] // TURN_RATE[1])
         scatter_lag = 1 + (chips - 1) * SCATTER_LAG
-        scatter_slots = scatter_lag + 3
+        scatter_slots = scatter_lag + 1
         stream = per // 2
         turn_at, out_at = [], []
         for q in range(QUERY_CHUNKS):
@@ -49,14 +51,14 @@
         ticks = out_at[-1] + n + scatter_lag
 
         def kernel(
-            selected, gradient, in_basis, eigen_rows, eigen_cols, out,
-            grad_tile, mine, other, swapped, arrived, crossed, sent, rows_w,
+            layer, ids, gradient, out_basis, in_basis, out_eigen, in_eigen, out,
+            selected, out_row, in_row, eigen_sum, eigen_rows, pick_tile, grad_tile, mine, other, swapped, arrived, crossed, sent, rows_w,
             turn_tile, part, staged, *rest,
         ):
             got, rest = rest[:bits], rest[bits:]
             (
                 scaled, out_tile, omine, oother, oswapped, rsent, lsent, rgot, lgot,
-                grad_sem, turn_sem, tile_sem,
+                pick_sem, grad_sem, turn_sem, tile_sem,
                 swap_s, swap_r, in_s, in_r, mid_s, mid_r, out_s, out_r, back_s, back_r,
                 red_s, red_r, all_s, all_r,
                 oswap_s, oswap_r, right_s, right_r, left_s, left_r,
@@ -169,9 +171,6 @@
                 greet(across(0, k))
             pl.when(chip > 0)(lambda: greet({"loop": me - 2}))
             pl.when(chip < chips - 1)(lambda: greet({"loop": me + 2}))
-            edge = (chip == 0) | (chip == chips - 1)
-            pl.semaphore_wait(barrier, 1 + bits + jnp.where(edge, 1, 2))
-
             def fetch_grad(g):
                 return pltpu.make_async_copy(
                     gradient.at[:, span(g % n, wide)], grad_tile.at[g % BUFFERS], grad_sem.at[g % BUFFERS]
@@ -179,22 +178,54 @@
 
             def fetch_turn(g):
                 return pltpu.make_async_copy(
-                    in_basis.at[:, span(g % n, thin)], turn_tile.at[g % BUFFERS], turn_sem.at[g % BUFFERS]
+                    in_basis.at[:, span(g % n, thin)], turn_tile.at[g % TURN_BUFFERS], turn_sem.at[g % TURN_BUFFERS]
                 )
 
             def fetch_out(g):
                 return pltpu.make_async_copy(
-                    in_basis.at[span(g % n, wide)], out_tile.at[g % BUFFERS], tile_sem.at[g % BUFFERS]
-                )
-
-            def ahead(fetch, g):
+                    in_basis.at[span(g % n, wide)], out_tile.at[g % OUT_BUFFERS], tile_sem.at[g % OUT_BUFFERS]
+                )
+
+            def fetch_pick(g):
+                return pltpu.make_async_copy(
+                    out_basis.at[:, span(g % picks, wide)],
+                    pick_tile.at[g % PICK_BUFFERS], pick_sem.at[g % PICK_BUFFERS],
+                )
+
+            def ahead(fetch, g, buffers, total=total):
                 fetch(g).wait()
-                more = g + BUFFERS - 1
+                more = g + buffers - 1
                 pl.when(more < total)(lambda: fetch(more).start())
+
+            def pick(g):
+                q, k = g // picks, g % picks
+                ahead(fetch_pick, g, PICK_BUFFERS, QUERY_CHUNKS * picks)
+                at = lax.broadcasted_iota(jnp.int32, (per, wide), 1) + k * wide
+                hot = ids[q] == at
+                values = lax.dot_general(
+                    hot.astype(bf16), pick_tile[g % PICK_BUFFERS], (((1,), (1,)), ((), ())),
+                    preferred_element_type=f32,
+                ).astype(bf16)
+                eigen = jnp.where(hot, out_row[:, span(k, wide)], 0.0)
+                eigen = sum(eigen[:, c : c + 128] for c in range(0, wide, 128))
+
+                @pl.when(k == 0)
+                def _():
+                    selected[q] = values
+                    eigen_sum[...] = eigen
+
+                @pl.when(k > 0)
+                def _():
+                    selected[q] += values
+                    eigen_sum[...] += eigen
+
+                @pl.when(k == picks - 1)
+                def _():
+                    eigen_rows[q] = jnp.sum(eigen_sum[...], axis=1, keepdims=True)
 
             def rows_tile(g):
                 s = g % sum_slots
-                ahead(fetch_grad, g)
+                ahead(fetch_grad, g, BUFFERS)
                 whole = jnp.dot(
                     selected[g // n], grad_tile[g % BUFFERS], preferred_element_type=f32
                 )
@@ -259,13 +290,13 @@
 
             def turn_tile_of(g):
                 s = g % red_slots
-                ahead(fetch_turn, g)
+                ahead(fetch_turn, g, TURN_BUFFERS)
                 cut = rows // DEPTHS
 
                 def some(j):
                     at = span(j, cut)
                     return jnp.dot(
-                        rows_w[g // n, :, at], turn_tile[g % BUFFERS, at], preferred_element_type=f32
+                        rows_w[g // n, :, at], turn_tile[g % TURN_BUFFERS, at], preferred_element_type=f32
                     )
 
                 part[s] = some(0)
@@ -290,7 +321,7 @@
                         pl.when(g >= red_slots)(
                             lambda turn=turn: all_send(g - red_slots, turn, k).wait_send()
                         )
-                        scale = eigen_rows[g // n, at] * eigen_cols[:, cut]
+                        scale = eigen_rows[g // n, at] * in_row[:, cut]
                         scaled[g // n, at, cut] = (value / (scale + damping)).astype(bf16)
                         all_send(g, turn, k).start()
                 if k + 1 < bits:
@@ -307,10 +338,10 @@
 
             def out_tile_of(g):
                 s = g % scatter_slots
-                ahead(fetch_out, g)
+                ahead(fetch_out, g, OUT_BUFFERS)
                 pl.when(g >= scatter_slots)(lambda: out_swap(g - scatter_slots).wait_send())
                 whole = lax.dot_general(
-                    scaled[g // n], out_tile[g % BUFFERS], (((1,), (1,)), ((), ())),
+                    scaled[g // n], out_tile[g % OUT_BUFFERS], (((1,), (1,)), ((), ())),
                     preferred_element_type=f32,
                 )
                 omine[s] = whole[:own]
@@ -367,13 +398,26 @@
                     lo, hi = jnp.minimum(first(u), n), jnp.minimum(first(u + 1), n)
                     each(lo + q * n, hi + q * n, f)
 
-            for g in range(BUFFERS - 1):
-                for fetch in (fetch_grad, fetch_turn, fetch_out):
+            def begin(fetch, buffers):
+                for g in range(buffers - 1):
                     fetch(g).start()
 
+            begin(fetch_pick, PICK_BUFFERS)
+            begin(fetch_grad, BUFFERS)
+            out_row[...] = out_eigen[pl.ds(layer[0], 1)]
+            in_row[...] = in_eigen[pl.ds(layer[0], 1)]
+            each(0, picks, pick)
+            begin(fetch_turn, TURN_BUFFERS)
+            begin(fetch_out, OUT_BUFFERS)
+            edge = (chip == 0) | (chip == chips - 1)
+            pl.semaphore_wait(barrier, 1 + bits + jnp.where(edge, 1, 2))
             row_at = [q * n for q in range(QUERY_CHUNKS)]
 
+            share = -(-picks * (QUERY_CHUNKS - 1) // (n - 1))
+
             def tick(t):
+                start = jnp.minimum(picks + t * share, QUERY_CHUNKS * picks)
+                each(start, jnp.minimum(start + share, QUERY_CHUNKS * picks), pick)
                 when(t, row_at, 0, rows_tile)
                 when(t, turn_at, 0, turn_tile_of)
                 when(t, out_at, 0, out_tile_of)
@@ -426,6 +470,7 @@
 
         vmem = pl.BlockSpec(memory_space=pltpu.VMEM)
         hbm = pl.BlockSpec(memory_space=pl.ANY)
+        smem = pl.BlockSpec(memory_space=pltpu.SMEM)
 
         def sems(count):
             return pltpu.SemaphoreType.DMA((count,))
@@ -436,24 +481,33 @@
         return pl.pallas_call(
             kernel,
             out_shape=jax.ShapeDtypeStruct((QUERY_CHUNKS * r, rows), bf16),
-            in_specs=[vmem, hbm, hbm, vmem, vmem],
+            in_specs=[smem, vmem, hbm, hbm, hbm, vmem, vmem],
             out_specs=vmem,
-            scratch_shapes=[slots(BUFFERS, depth, wide), pltpu.VMEM((sum_slots, own, wide), f32)]
+            scratch_shapes=[
+                slots(QUERY_CHUNKS, per, depth),
+                pltpu.VMEM((1, units), f32),
+                pltpu.VMEM((1, cols), f32),
+                pltpu.VMEM((per, 128), f32),
+                pltpu.VMEM((QUERY_CHUNKS, per, 1), f32),
+                slots(PICK_BUFFERS, depth, wide),
+                slots(BUFFERS, depth, wide),
+            ]
+            + [pltpu.VMEM((sum_slots, own, wide), f32)]
             + [slots(sum_slots, own, wide)] * 5
             + [
                 slots(QUERY_CHUNKS, per, rows),
-                slots(BUFFERS, rows, thin),
+                slots(TURN_BUFFERS, rows, thin),
                 pltpu.VMEM((red_slots, per, thin), f32),
                 slots(red_slots, per, thin),
             ]
             + [slots(red_slots, 2, stream >> (k + 1), thin) for k in range(bits)]
             + [
                 slots(QUERY_CHUNKS, per, cols),
-                slots(BUFFERS, wide, cols),
+                slots(OUT_BUFFERS, wide, cols),
                 pltpu.VMEM((scatter_slots, own, wide), f32),
             ]
             + [slots(scatter_slots, own, wide)] * 6
-            + [sems(BUFFERS)] * 3
+            + [sems(PICK_BUFFERS), sems(BUFFERS), sems(TURN_BUFFERS), sems(OUT_BUFFERS)]
             + [sems(sum_slots)] * 10
             + [sems(2 * bits * red_slots)] * 4
             + [sems(scatter_slots)] * 2
@@ -472,17 +526,10 @@
         per = queries // QUERY_CHUNKS
         ids = query_ids.reshape(chips, 2, QUERY_CHUNKS, r).transpose(2, 1, 0, 3)
         ids = jnp.where(core == 0, ids, ids[:, ::-1]).reshape(-1)
-        out_row = lax.dynamic_index_in_dim(out_eigen, layer_index[0], 0, keepdims=False)
-        eigen_cols = lax.dynamic_index_in_dim(in_eigen, layer_index[0], 0)
-        eigen_rows = jnp.take(out_row, ids).reshape(QUERY_CHUNKS, per, 1)
-        every = lax.broadcasted_iota(jnp.int32, (queries, out_basis.shape[1]), 1)
-        selected = lax.dot_general(
-            (ids[:, None] == every).astype(bf16), out_basis,
-            (((1,), (1,)), ((), ())), preferred_element_type=f32,
-        ).astype(bf16)
-        selected = selected.reshape(QUERY_CHUNKS, per, depth)
-        run = product(per, per // 2, r, depth, rows, cols, piece_count(rows, cols))
-        return run(selected, gradient, in_basis, eigen_rows, eigen_cols)
+        ids = ids.reshape(QUERY_CHUNKS, per, 1)
+        units = out_basis.shape[1]
+        run = product(per, per // 2, r, depth, units, rows, cols, piece_count(rows, cols))
+        return run(layer_index, ids, gradient, out_basis, in_basis, out_eigen, in_eigen)
 
     return per_device
 

time: 225 us -> 216 us (0.960)
  matrix products: 12.9 us -> 0 us
  Pallas kernels: 202 us -> 210 us
  local copies, waits for them, and re-layouts: 8.17 us -> 3.9 us
    dot_general x1 -> x0, matrix products: 12.9 us -> none  [per_device(): lax.dot_general((ids[:, None] == every).astype(bf16), out_basis, (((1,),...]
    pallas_call x1, Pallas kernels: 202 us -> 210 us  [per_device(): run(layer_index, ids, gradient, out_basis, in_basis, out_eigen, in_eigen)]
    gather x2 -> x0, local copies, waits for them, and re-layouts: 3.35 us -> none  [per_device(): eigen_rows = jnp.take(out_row, ids).reshape(QUERY_CHUNKS, per, 1)]
where the time goes in v2:
time: 216 us; the launch traced here: 215 us
  Pallas kernels  210 us (97%)
  local copies, waits for them, and re-layouts  3.9 us (2%)
    pallas_call x1, Pallas kernels, per_device(): run(layer_index, ids, gradient, out_basis, in_basis, out_eigen, in_eigen)  210 us

profile of v2, /device:TPU:0, one launch (start us, length us, event | category | flops | bytes accessed | tf_op | source)
XLA Modules:
  0.0 214.7 jit_solution(9259053449341398910)
XLA Ops:
  0.7 0.8 reshape.3
  1.4 1.0 reshape_reshape.4.ids
  2.4 210.2 %shard_map.73 = bf16[64,7168]{1,0:T(8,128)(2,1)} custom-call(s32[1]{0:T(128)S(6)} %copy.11.layer, s32[2,256,1]{2,1,0:T(8,128)} %reshape_reshape.4.ids, bf16[1024,7168]{1,0:T(8,128)(2,1)} %gradient.1, bf16[1024,8192]{1,0:T(8,128)(2,1)} %out_basis.1, bf16[7168,3584]{1,0:T(8,128)(2,1)} %in_basis.1, f32[4,8192]{1,0:T(4,128)} %out_eigen.1, f32[4,3584]{1,0:T(4,128)} %in_eigen.1), custom_call_target="tpu_custom_call" | custom-call | tf_op jit(solution)/shard_map/pallas_call | solution.py:532
  212.6 2.2 %copy.12 = bf16[64,7168]{1,0:T(8,128)(2,1)} copy(bf16[64,7168]{1,0:T(8,128)(2,1)} %shard_map.73) | data formatting | bytes 1835008
  (2 shorter events, 0.0 us)

commit v3 on v2

--- a/solution.py
+++ b/solution.py
@@ -10,9 +10,9 @@
 PIECES = 14
 IN_LAG, MID_LAG, OUT_LAG, SCATTER_LAG = 2, 2, 2, 2
 BUFFERS = 3
-PICK_BUFFERS, TURN_BUFFERS, OUT_BUFFERS = 6, 3, 2
+PICK_BUFFERS, TURN_BUFFERS, OUT_BUFFERS = 4, 2, 2
+PICK_WIDE = 1024
 DEPTHS = 2
-TURN_RATE = (1, 1)
 RED_LAG = 2
 
 
@@ -33,20 +33,20 @@
     def product(per, own, r, depth, units, rows, cols, n):
         wide, thin = rows // n, cols // n
         total = QUERY_CHUNKS * n
-        picks = units // wide
+        pick_wide = min(PICK_WIDE, units)
+        picks = units // pick_wide
         sum_lag = 2 + (IN_LAG + OUT_LAG) * (half - 1) + MID_LAG
         sum_slots = sum_lag + 1
         red_lag = 2 * bits * RED_LAG
-        red_slots = -(-(red_lag + 1) * TURN_RATE[0] // TURN_RATE[1])
+        red_slots = red_lag + 1
         scatter_lag = 1 + (chips - 1) * SCATTER_LAG
         scatter_slots = scatter_lag + 1
         stream = per // 2
         turn_at, out_at = [], []
         for q in range(QUERY_CHUNKS):
             ready = (q + 1) * n + sum_lag
-            turn_at.append(ready)
-            num, den = (1, 1) if q else TURN_RATE
-            ready = turn_at[-1] + -(-n * den // num) + red_lag
+            turn_at.append(max(ready, turn_at[-1] + n) if q else ready)
+            ready = turn_at[-1] + n + red_lag
             out_at.append(max(ready, out_at[-1] + n) if q else ready)
         ticks = out_at[-1] + n + scatter_lag
 
@@ -188,7 +188,7 @@
 
             def fetch_pick(g):
                 return pltpu.make_async_copy(
-                    out_basis.at[:, span(g % picks, wide)],
+                    out_basis.at[:, span(g % picks, pick_wide)],
                     pick_tile.at[g % PICK_BUFFERS], pick_sem.at[g % PICK_BUFFERS],
                 )
 
@@ -200,14 +200,14 @@
             def pick(g):
                 q, k = g // picks, g % picks
                 ahead(fetch_pick, g, PICK_BUFFERS, QUERY_CHUNKS * picks)
-                at = lax.broadcasted_iota(jnp.int32, (per, wide), 1) + k * wide
+                at = lax.broadcasted_iota(jnp.int32, (per, pick_wide), 1) + k * pick_wide
                 hot = ids[q] == at
                 values = lax.dot_general(
                     hot.astype(bf16), pick_tile[g % PICK_BUFFERS], (((1,), (1,)), ((), ())),
                     preferred_element_type=f32,
                 ).astype(bf16)
-                eigen = jnp.where(hot, out_row[:, span(k, wide)], 0.0)
-                eigen = sum(eigen[:, c : c + 128] for c in range(0, wide, 128))
+                eigen = jnp.where(hot, out_row[:, span(k, pick_wide)], 0.0)
+                eigen = sum(eigen[:, c : c + 128] for c in range(0, pick_wide, 128))
 
                 @pl.when(k == 0)
                 def _():
@@ -389,14 +389,11 @@
 
             def when(t, starts, lag, f):
                 u = t - lag
-                for q in range(QUERY_CHUNKS):
-                    num, den = TURN_RATE if starts is turn_at and q == 0 else (1, 1)
-
-                    def first(u):
-                        return jnp.clip(u - starts[q], 0, n) * num // den
-
-                    lo, hi = jnp.minimum(first(u), n), jnp.minimum(first(u + 1), n)
-                    each(lo + q * n, hi + q * n, f)
+                i, g = u - starts[0], u - starts[0]
+                for q in range(1, QUERY_CHUNKS):
+                    i = jnp.where(u >= starts[q], u - starts[q], i)
+                    g = jnp.where(u >= starts[q], u - starts[q] + q * n, g)
+                pl.when((i >= 0) & (i < n))(lambda: f(g))
 
             def begin(fetch, buffers):
                 for g in range(buffers - 1):
@@ -489,7 +486,7 @@
                 pltpu.VMEM((1, cols), f32),
                 pltpu.VMEM((per, 128), f32),
                 pltpu.VMEM((QUERY_CHUNKS, per, 1), f32),
-                slots(PICK_BUFFERS, depth, wide),
+                slots(PICK_BUFFERS, depth, pick_wide),
                 slots(BUFFERS, depth, wide),
             ]
             + [pltpu.VMEM((sum_slots, own, wide), f32)]

time: 216 us -> 212 us (0.981)
  Pallas kernels: 210 us -> 206 us
    pallas_call x1, Pallas kernels: 210 us -> 206 us  [per_device(): run(layer_index, ids, gradient, out_basis, in_basis, out_eigen, in_eigen)]
where the time goes in v3:
time: 212 us; the launch traced here: 211 us
  Pallas kernels  206 us (97%)
  local copies, waits for them, and re-layouts  3.9 us (2%)
    pallas_call x1, Pallas kernels, per_device(): run(layer_index, ids, gradient, out_basis, in_basis, out_eigen, in_eigen)  206 us

profile of v3, /device:TPU:0, one launch (start us, length us, event | category | flops | bytes accessed | tf_op | source)
XLA Modules:
  0.0 210.7 jit_solution(13228538583787681081)
XLA Ops:
  0.7 0.8 reshape.3
  1.4 1.0 reshape_reshape.4.ids
  2.4 206.1 %shard_map.73 = bf16[64,7168]{1,0:T(8,128)(2,1)} custom-call(s32[1]{0:T(128)S(6)} %copy.11.layer, s32[2,256,1]{2,1,0:T(8,128)} %reshape_reshape.4.ids, bf16[1024,7168]{1,0:T(8,128)(2,1)} %gradient.1, bf16[1024,8192]{1,0:T(8,128)(2,1)} %out_basis.1, bf16[7168,3584]{1,0:T(8,128)(2,1)} %in_basis.1, f32[4,8192]{1,0:T(4,128)} %out_eigen.1, f32[4,3584]{1,0:T(4,128)} %in_eigen.1), custom_call_target="tpu_custom_call" | custom-call | tf_op jit(solution)/shard_map/pallas_call | solution.py:529
  208.5 2.2 %copy.12 = bf16[64,7168]{1,0:T(8,128)(2,1)} copy(bf16[64,7168]{1,0:T(8,128)(2,1)} %shard_map.73) | data formatting | bytes 1835008
  (2 shorter events, 0.0 us)

commit v4 on v3

--- a/solution.py
+++ b/solution.py
@@ -10,8 +10,8 @@
 PIECES = 14
 IN_LAG, MID_LAG, OUT_LAG, SCATTER_LAG = 2, 2, 2, 2
 BUFFERS = 3
-PICK_BUFFERS, TURN_BUFFERS, OUT_BUFFERS = 4, 2, 2
-PICK_WIDE = 1024
+PICK_BUFFERS, TURN_BUFFERS, OUT_BUFFERS = 2, 2, 2
+PICK_WIDE = 2048
 DEPTHS = 2
 RED_LAG = 2
 

time: 212 us -> 217 us (1.024)
  Pallas kernels: 206 us -> 211 us
    pallas_call x1, Pallas kernels: 206 us -> 211 us  [per_device(): run(layer_index, ids, gradient, out_basis, in_basis, out_eigen, in_eigen)]
where the time goes in v4:
time: 217 us; the launch traced here: 216 us
  Pallas kernels  211 us (97%)
  local copies, waits for them, and re-layouts  3.9 us (2%)
    pallas_call x1, Pallas kernels, per_device(): run(layer_index, ids, gradient, out_basis, in_basis, out_eigen, in_eigen)  211 us

profile of v4, /device:TPU:0, one launch (start us, length us, event | category | flops | bytes accessed | tf_op | source)
XLA Modules:
  0.0 215.7 jit_solution(15921529733763737325)
XLA Ops:
  0.7 0.8 reshape.3
  1.4 1.0 reshape_reshape.4.ids
  2.4 211.1 %shard_map.73 = bf16[64,7168]{1,0:T(8,128)(2,1)} custom-call(s32[1]{0:T(128)S(6)} %copy.11.layer, s32[2,256,1]{2,1,0:T(8,128)} %reshape_reshape.4.ids, bf16[1024,7168]{1,0:T(8,128)(2,1)} %gradient.1, bf16[1024,8192]{1,0:T(8,128)(2,1)} %out_basis.1, bf16[7168,3584]{1,0:T(8,128)(2,1)} %in_basis.1, f32[4,8192]{1,0:T(4,128)} %out_eigen.1, f32[4,3584]{1,0:T(4,128)} %in_eigen.1), custom_call_target="tpu_custom_call" | custom-call | tf_op jit(solution)/shard_map/pallas_call | solution.py:529
  213.5 2.2 %copy.12 = bf16[64,7168]{1,0:T(8,128)(2,1)} copy(bf16[64,7168]{1,0:T(8,128)(2,1)} %shard_map.73) | data formatting | bytes 1835008
  (2 shorter events, 0.0 us)
